TPU v7x, 256 devices: a whole 4x4x8 slice. The times are simulated.
256 devices in a mesh: freq: 8 (over x, core), mode: 32 (over y, z).
Axes of the slice: x: 4, y: 4, z: 8, core: 2. Of those that a mesh axis runs over, the one named last changes fastest.
Arguments:
- mode_shapes: bfloat16 [6144, 12288], P(None, 'mode'), may hold values from -0.109375 to 0.109375
- modal_freq: float32 [12288], P('mode'), may hold values from 0.5 to 4
- damping: float32 [12288], P('mode'), may hold values from 0.05 to 0.2
- excitation: float32 [32], P('freq'), parts along dimension 0, may hold values from 0.5 to 4
- modal_load: float32 [12288, 32, 2, 64], P('mode', 'freq'), parts along dimension 1, may hold values from -6 to 6
- attach: int32 [32, 96], replicated, may hold values from 0 to 6143
- row_count: int32 [32], P('mode'), may hold values from 48 to 384, as said below
- otm: bfloat16 [32, 384, 96], P('mode'), may hold values from -0.625 to 0.625
Outputs:
- csd: bfloat16 [32, 32, 2, 384, 384], P('mode', 'freq'), parts along dimension 1
- joint_csd: bfloat16 [32, 32, 2, 128, 384], P('mode', 'freq'), parts along dimension 1
There are 8 independent parts, one for each index of `freq`. A program takes and returns all parts, laid end to end along the dimension named above; an argument that names none is the same for every part. Nothing has to cross between parts.
Inputs may be any that keep to these rules, and one draw needn't show every extreme that they name: `row_count`: at least one component has exactly 384 rows in every draw.
All inputs are finite; a program needn't handle non-finite values.
Results may differ from a plain program's by a relative error of at most 0.008.
Values may be sent and summed in bfloat16 or wider, within the bound.
A program may use at most 128 MiB of HBM per device.

v0:
```python
import jax
import jax.numpy as jnp
from jax import lax
from jax.sharding import PartitionSpec as P

CROSS = 128


def shifted(value, axis, steps):
    count = lax.axis_size(axis)
    initial, last = (max(0, -steps), min(count, count - steps))
    return lax.ppermute(value, axis, [(source, source + steps) for source in range(initial, last)])


def per_device(mode_shapes, modal_freq, damping, excitation, modal_load, attach, row_count, otm):
    comp_here = otm.shape[0]
    rows_max = otm.shape[1]
    att_len = otm.shape[2]
    lines = excitation.shape[0]
    width = modal_load.shape[3]
    columns = lines * 2 * width
    omega_sq = modal_freq * modal_freq
    real_part = omega_sq[:, None] - (excitation * excitation)[None, :]
    imag_part = 2.0 * damping[:, None] * modal_freq[:, None] * excitation[None, :]
    denom = real_part * real_part + imag_part * imag_part
    frf_re = (omega_sq[:, None] * real_part / denom)[:, :, None]
    frf_im = (-omega_sq[:, None] * imag_part / denom)[:, :, None]
    load_re = modal_load[:, :, 0, :]
    load_im = modal_load[:, :, 1, :]
    resp_re = frf_re * load_re - frf_im * load_im
    resp_im = frf_re * load_im + frf_im * load_re
    modal_resp = jnp.stack([resp_re, resp_im], axis=2).astype(jnp.bfloat16)
    modal_resp = modal_resp.reshape(modal_resp.shape[0], columns)
    flat_attach = attach.reshape(-1)
    own_start = lax.axis_index("mode") * (comp_here * att_len)
    band = lax.psum_scatter(
        jnp.dot(mode_shapes, modal_resp, preferred_element_type=jnp.float32),
        "mode",
        scatter_dimension=0,
        tiled=True,
    ).astype(jnp.bfloat16)
    whole = lax.all_gather(band, "mode", axis=0, tiled=True)
    index_rows = lax.dynamic_slice_in_dim(flat_attach, own_start, comp_here * att_len)
    picked = jnp.take(whole, index_rows, axis=0)
    picked = picked.reshape(comp_here, att_len, columns)
    row_mask = jnp.arange(rows_max, dtype=jnp.int32)[None, :] < row_count[:, None]
    masked_otm = jnp.where(row_mask[:, :, None], otm, jnp.zeros_like(otm))
    factor = jnp.einsum(
        "cra,caj->crj", masked_otm, picked, preferred_element_type=jnp.float32
    ).astype(jnp.bfloat16)
    zmat = factor.reshape(comp_here, rows_max, lines, 2 * width)
    wmat = jnp.concatenate([zmat[..., width:], -zmat[..., :width]], axis=-1)
    following = shifted(zmat[0], "mode", -1)
    partner = jnp.concatenate([zmat[1:], following[None]], axis=0)
    block = 128
    z_here = zmat[0]
    w_here = wmat[0]
    needed = (row_count[0] + block - 1) // block

    def block_step(step, buffer):
        z_rows = lax.dynamic_slice_in_dim(z_here, step * block, block, 0)
        w_rows = lax.dynamic_slice_in_dim(w_here, step * block, block, 0)
        part_re = (
            jnp.einsum("rfk,sfk->frs", z_rows, z_here, preferred_element_type=jnp.float32) / width
        )
        part_im = (
            jnp.einsum("rfk,sfk->frs", w_rows, z_here, preferred_element_type=jnp.float32) / width
        )
        value = jnp.stack([part_re, part_im], axis=1).astype(jnp.bfloat16)
        zero = jnp.zeros((), jnp.int32)
        return lax.dynamic_update_slice(
            buffer, value, (zero, zero, (step * block).astype(jnp.int32), zero)
        )

    empty = jnp.zeros((lines, 2, rows_max, rows_max), jnp.bfloat16)
    auto_blocks = [lax.fori_loop(0, needed, block_step, empty)]
    csd = jnp.stack(auto_blocks, axis=0)
    joint_re = (
        jnp.einsum("crfk,csfk->cfrs", zmat[:, :CROSS], partner, preferred_element_type=jnp.float32)
        / width
    )
    joint_im = (
        jnp.einsum("crfk,csfk->cfrs", wmat[:, :CROSS], partner, preferred_element_type=jnp.float32)
        / width
    )
    joint_csd = jnp.stack([joint_re, joint_im], axis=2).astype(jnp.bfloat16)
    return (csd, joint_csd)


def solution(mesh):
    return jax.shard_map(
        per_device,
        mesh=mesh,
        in_specs=(
            P(None, "mode"),
            P("mode"),
            P("mode"),
            P("freq"),
            P("mode", "freq", None, None),
            P(),
            P("mode"),
            P("mode", None, None),
        ),
        out_specs=(P("mode", "freq", None, None, None), P("mode", "freq", None, None, None)),
        check_vma=False,
    )
```

profile of v0, /device:TPU:16, one launch (start us, length us, event | category | flops | bytes accessed | tf_op | source)
XLA Modules:
  0.0 393.1 jit_solution(15512524188562069523)
XLA Ops:
  7.2 0.7 mul.124
  7.9 0.7 multiply_multiply_fusion.2
  8.6 0.7 fusion.22
  9.4 1.2 subtract_convert_fusion
  10.7 8.7 %convolution_bitcast_fusion = f32[6144,512]{0,1:T(8,128)} fusion(bf16[384,512]{0,1:T(8,128)(2,1)S(1)} %bitcast.55, bf16[6144,384]{1,0:T(8,128)(2,1)} %param.10), kind=kOutput, calls=%fused_computation.13 | convolution fusion | flops 2415919104 | bytes 17694720 | tf_op jit(solution)/shard_map/dot_general | solution.py:37
  19.4 12.6 %copy.34 = f32[6144,512]{1,0:T(8,128)} copy(f32[6144,512]{0,1:T(8,128)} %convolution_bitcast_fusion) | data formatting | bytes 25165824
  32.1 239.8 %reduce-scatter.4.cloned.1.call-done = f32[192,512]{1,0:T(8,128)} async-done(((f32[6144,512]{1,0:T(8,128)}), f32[192,512]{1,0:T(8,128)}) %reduce-scatter.4.cloned.1.call-update) | async-done | bytes 393232 | tf_op jit(solution)/shard_map/reduce_scatter | solution.py:36
  271.8 1.7 convert_element_type.23
  274.3 0.1 compare_and_fusion
  274.4 87.0 %all-gather.2.cloned.1.call-done = bf16[6144,512]{1,0:T(8,128)(2,1)} async-done(((bf16[192,512]{1,0:T(8,128)(2,1)}), bf16[6144,512]{1,0:T(8,128)(2,1)}) %all-gather.2.cloned.1.call-update) | async-done | bytes 6291472 | tf_op jit(solution)/shard_map/all_gather | solution.py:42
  361.4 4.4 %gather_fusion = bf16[96,512]{1,0:T(8,128)(2,1)S(1)} fusion(bf16[6144,512]{1,0:T(8,128)(2,1)} %all-gather.2.cloned.1.call-done, s32[1024]{0:T(1024)S(1)} %pad_clamp_fusion), kind=kCustom, calls=%fused_computation | custom fusion | bytes 196992 | tf_op jit(solution)/shard_map/jit(_take)/gather | solution.py:44
  365.8 0.3 convolution_convert_fusion
  366.2 0.1 reshape.262
  366.3 0.8 copy_bitcast_fusion
  367.1 0.4 fusion.28
  367.6 4.1 %collective-permute-start = (bf16[384,4,128]{2,0,1:T(8,128)(2,1)}, bf16[384,4,128]{2,0,1:T(8,128)(2,1)S(1)}, u32[]{:S(2)}, u32[]{:S(2)}) collective-permute-start(bf16[384,4,128]{2,0,1:T(8,128)(2,1)} %copy_bitcast_fusion), channel_id=1, source_target_pairs={{1,0},{2,1},{3,2},{4,3},{5,4},{6,5},{7,6},{8,7},{9,8},{10,9},{11,1... | collective-permute-start | bytes 1179656 | tf_op jit(solution)/shard_map/ppermute | solution.py:12
  371.7 0.2 maximum_bitcast_fusion
  371.9 1.6 broadcast_in_dim.21.clone
  373.5 11.0 %while.10 = (s32[]{:T(128)}, bf16[4,2,384,384]{3,2,1,0:T(8,128)(2,1)}, s32[]{:T(128)}, bf16[384,4,128]{2,0,1:T(8,128)(2,1)}, bf16[384,4,128]{2,0,1:T(8,128)(2,1)...) while((s32[]{:T(128)}, bf16[4,2,384,384]{3,2,1,0:T(8,128)(2,1)}, s32[]{:T(128)}, ...), condition=%wide.region_2.3_spmd, body=%wide.region_1.2_spmd.sunk | while | flops 101842944 | bytes 3408023 | solution.py:76
  373.5 1.3 fusion.46
  374.8 1.4 fusion.47
  376.2 1.0 copy_dynamic-update-slice_fusion.2
  377.2 1.3 fusion.46
  378.5 1.4 fusion.47
  379.9 1.0 copy_dynamic-update-slice_fusion.2
  380.9 1.3 fusion.46
  382.2 1.4 fusion.47
  383.5 1.0 copy_dynamic-update-slice_fusion.2
  384.6 0.3 fusion.10
  384.9 0.3 fusion.11
  385.2 0.1 pad_maximum_fusion.1
  385.3 1.0 copy.33
  (16 shorter events, 0.4 us)
Async XLA Ops:
  7.2 264.7 %reduce-scatter.4.cloned.1.call-start = ((), (), s32[]{:S(2)}) async-start(), calls=%async_computation.2 | async-start | bytes 12976128 | tf_op jit(solution)/shard_map/reduce_scatter | solution.py:36
  32.0 242.2 %copy-start.1 = (s32[32,96]{1,0:T(8,128)S(1)}, s32[32,96]{1,0:T(8,128)}, u32[]{:S(2)}) copy-start(s32[32,96]{1,0:T(8,128)} %param.15) | copy-start | bytes 36868
  32.0 333.9 %copy-start = (bf16[1,384,96]{1,2,0:T(8,128)(2,1)S(1)}, bf16[1,384,96]{1,2,0:T(8,128)(2,1)}, u32[]{:S(2)}) copy-start(bf16[1,384,96]{1,2,0:T(8,128)(2,1)} %param.17) | copy-start | bytes 221188
  32.0 329.4 %all-gather.2.cloned.1.call-start = ((), (), s32[]{:S(2)}) async-start(), calls=%async_computation.1 | async-start | bytes 6488064 | tf_op jit(solution)/shard_map/all_gather | solution.py:42
  367.6 17.0 %collective-permute-start = (bf16[384,4,128]{2,0,1:T(8,128)(2,1)}, bf16[384,4,128]{2,0,1:T(8,128)(2,1)S(1)}, u32[]{:S(2)}, u32[]{:S(2)}) collective-permute-start(bf16[384,4,128]{2,0,1:T(8,128)(2,1)} %copy_bitcast_fusion), channel_id=1, source_target_pairs={{1,0},{2,1},{3,2},{4,3},{5,4},{6,5},{7,6},{8,7},{9,8},{10,9},{11,1... | collective-permute-start | bytes 1179656 | tf_op jit(solution)/shard_map/ppermute | solution.py:12
Sparse Core Ops, SparseCore 0:
  32.1 239.6 reduce-scatter.3
  275.0 86.3 all-gather.1
where the time goes:
time: 394 us; the launch traced here: 393 us
  waiting for transfers between devices  327 us (83%)
  local copies, waits for them, and re-layouts  21 us (5%)
  matrix products  17.8 us (5%)
  between operations  14.8 us (4%)
  other arithmetic  8.52 us (2%)
  starting transfers between devices  4.16 us (1%)
    reduce_scatter x1, waiting for transfers between devices, per_device(): lax.psum_scatter(jnp.dot(mode_shapes, modal_resp, preferred_element_type=...  240 us
    all_gather x1, waiting for transfers between devices, per_device(): whole = lax.all_gather(band, 'mode', axis=0, tiled=True)  87 us
    unnamed x7, local copies, waits for them, and re-layouts  13.6 us
    dot_general x1, matrix products, per_device(): jnp.dot(mode_shapes, modal_resp, preferred_element_type=jnp.float32)  8.73 us
  transfers between devices with their start and end apart: 3, of which 2 were waited for; matrix products, arithmetic and copies ran while one was open for 3% of the time, Pallas kernels for 0%

commit v1 on v0

--- a/solution.py
+++ b/solution.py
@@ -39,7 +39,9 @@
         scatter_dimension=0,
         tiled=True,
     ).astype(jnp.bfloat16)
-    whole = lax.all_gather(band, "mode", axis=0, tiled=True)
+    whole = jnp.concatenate(
+        lax.all_to_all(jnp.stack([band] * lax.axis_size("mode")), "mode", 0, 0), axis=0
+    )
     index_rows = lax.dynamic_slice_in_dim(flat_attach, own_start, comp_here * att_len)
     picked = jnp.take(whole, index_rows, axis=0)
     picked = picked.reshape(comp_here, att_len, columns)

time: 394 us -> 453 us (1.15)
  waiting for transfers between devices: 327 us -> 374 us
  starting transfers between devices: 4.16 us -> 12 us
    all_to_all x0 -> x1, waiting for transfers between devices: none -> 134 us  [per_device(): lax.all_to_all(jnp.stack([band] * lax.axis_size('mode')), 'mode', 0, 0)]
    all_gather x1 -> x0, waiting for transfers between devices: 87 us -> none  [per_device(): whole = lax.all_gather(band, 'mode', axis=0, tiled=True)]
    all_to_all x0 -> x1, starting transfers between devices: none -> 8.3 us  [per_device(): lax.all_to_all(jnp.stack([band] * lax.axis_size('mode')), 'mode', 0, 0)]
where the time goes in v1:
time: 453 us; the launch traced here: 451 us
  waiting for transfers between devices  374 us (83%)
  local copies, waits for them, and re-layouts  24.4 us (5%)
  matrix products  17.8 us (4%)
  between operations  14.8 us (3%)
  starting transfers between devices  12 us (3%)
  other arithmetic  7.85 us (2%)
    reduce_scatter x1, waiting for transfers between devices, per_device(): lax.psum_scatter(jnp.dot(mode_shapes, modal_resp, preferred_element_type=...  240 us
    all_to_all x1, waiting for transfers between devices, per_device(): lax.all_to_all(jnp.stack([band] * lax.axis_size('mode')), 'mode', 0, 0)  134 us
    unnamed x7, local copies, waits for them, and re-layouts  13.6 us
  transfers between devices with their start and end apart: 3, of which 2 were waited for; matrix products, arithmetic and copies ran while one was open for 3% of the time, Pallas kernels for 0%

profile of v1, /device:TPU:16, one launch (start us, length us, event | category | flops | bytes accessed | tf_op | source)
XLA Modules:
  0.0 451.1 jit_solution(3956189446963652829)
XLA Ops:
  7.2 0.7 mul.124
  7.9 0.7 multiply_multiply_fusion.2
  8.6 0.7 fusion.22
  9.4 1.2 subtract_convert_fusion
  10.7 8.7 %convolution_bitcast_fusion = f32[6144,512]{0,1:T(8,128)} fusion(bf16[384,512]{0,1:T(8,128)(2,1)S(1)} %bitcast.56, bf16[6144,384]{1,0:T(8,128)(2,1)} %param.10), kind=kOutput, calls=%fused_computation.13 | convolution fusion | flops 2415919104 | bytes 17694720 | tf_op jit(solution)/shard_map/dot_general | solution.py:37
  19.4 12.6 %copy.34 = f32[6144,512]{1,0:T(8,128)} copy(f32[6144,512]{0,1:T(8,128)} %convolution_bitcast_fusion) | data formatting | bytes 25165824
  32.0 239.8 %reduce-scatter.4.cloned.1.call-done = f32[192,512]{1,0:T(8,128)} async-done(((f32[6144,512]{1,0:T(8,128)}), f32[192,512]{1,0:T(8,128)}) %reduce-scatter.4.cloned.1.call-update) | async-done | bytes 393232 | tf_op jit(solution)/shard_map/reduce_scatter | solution.py:36
  271.8 1.0 convert_element_type.23
  272.9 3.4 stack.23
  276.2 8.3 %all-to-all-start = ((bf16[32,192,512]{2,1,0:T(8,128)(2,1)}), bf16[32,192,512]{2,1,0:T(8,128)(2,1)}, u32[]{:S(2)}, u32[]{:S(2)}) async-start(bf16[32,192,512]{2,1,0:T(8,128)(2,1)} %stack.23), calls=%async_computation | async-start | bytes 12582912 | tf_op jit(solution)/shard_map/all_to_all | solution.py:43
  285.4 134.4 %all-to-all-done = bf16[32,192,512]{2,1,0:T(8,128)(2,1)} async-done(((bf16[32,192,512]{2,1,0:T(8,128)(2,1)}), bf16[32,192,512]{2,1,0:T(8,128)(2,1)}, u32[]{:S(2)}, u32[]{:S(2)}) %all-to-all-start) | async-done | bytes 6291488 | tf_op jit(solution)/shard_map/all_to_all | solution.py:43
  419.8 4.4 gather_fusion
  424.2 0.3 convolution_convert_fusion
  424.5 0.1 reshape.268
  424.6 0.8 copy_bitcast_fusion
  425.4 0.4 fusion.28
  425.9 3.7 collective-permute-start
  429.6 0.2 maximum_bitcast_fusion
  429.9 1.6 broadcast_in_dim.21.clone
  431.5 11.0 %while.10 = (s32[]{:T(128)}, bf16[4,2,384,384]{3,2,1,0:T(8,128)(2,1)}, s32[]{:T(128)}, bf16[384,4,128]{2,0,1:T(8,128)(2,1)}, bf16[384,4,128]{2,0,1:T(8,128)(2,1)...) while((s32[]{:T(128)}, bf16[4,2,384,384]{3,2,1,0:T(8,128)(2,1)}, s32[]{:T(128)}, ...), condition=%wide.region_2.3_spmd, body=%wide.region_1.2_spmd.sunk | while | flops 101842944 | bytes 3408023 | solution.py:78
  431.5 1.3 fusion.46
  432.8 1.4 fusion.47
  434.2 1.0 copy_dynamic-update-slice_fusion.2
  435.1 1.3 fusion.46
  436.4 1.4 fusion.47
  437.8 1.0 copy_dynamic-update-slice_fusion.2
  438.8 1.3 fusion.46
  440.1 1.4 fusion.47
  441.5 1.0 copy_dynamic-update-slice_fusion.2
  442.5 0.4 fusion.10
  442.9 0.3 fusion.11
  443.3 1.0 copy.33
  (16 shorter events, 0.5 us)
Async XLA Ops:
  7.2 264.7 %reduce-scatter.4.cloned.1.call-start = ((), (), s32[]{:S(2)}) async-start(), calls=%async_computation.2 | async-start | bytes 12976128 | tf_op jit(solution)/shard_map/reduce_scatter | solution.py:36
  276.2 9.0 %copy-start.1 = (s32[32,96]{1,0:T(8,128)S(1)}, s32[32,96]{1,0:T(8,128)}, u32[]{:S(2)}) copy-start(s32[32,96]{1,0:T(8,128)} %param.15) | copy-start | bytes 36868
  276.2 147.9 %copy-start = (bf16[1,384,96]{1,2,0:T(8,128)(2,1)S(1)}, bf16[1,384,96]{1,2,0:T(8,128)(2,1)}, u32[]{:S(2)}) copy-start(bf16[1,384,96]{1,2,0:T(8,128)(2,1)} %param.17) | copy-start | bytes 221188
  276.2 143.6 %all-to-all-start = ((bf16[32,192,512]{2,1,0:T(8,128)(2,1)}), bf16[32,192,512]{2,1,0:T(8,128)(2,1)}, u32[]{:S(2)}, u32[]{:S(2)}) async-start(bf16[32,192,512]{2,1,0:T(8,128)(2,1)} %stack.23), calls=%async_computation | async-start | bytes 12582912 | tf_op jit(solution)/shard_map/all_to_all | solution.py:43
  425.9 16.6 %collective-permute-start = (bf16[384,4,128]{2,0,1:T(8,128)(2,1)}, bf16[384,4,128]{2,0,1:T(8,128)(2,1)S(1)}, u32[]{:S(2)}, u32[]{:S(2)}) collective-permute-start(bf16[384,4,128]{2,0,1:T(8,128)(2,1)} %copy_bitcast_fusion), channel_id=1, source_target_pairs={{1,0},{2,1},{3,2},{4,3},{5,4},{6,5},{7,6},{8,7},{9,8},{10,9},{11,1... | collective-permute-start | bytes 1179656 | tf_op jit(solution)/shard_map/ppermute | solution.py:12
Sparse Core Ops, SparseCore 0:
  32.1 239.6 reduce-scatter.3
